TPU v7x, 32 devices: a whole 2x2x4 slice. The times are simulated.
32 devices in a mesh: ctx: 8 (over z, y), ch: 4 (over x, core).
Axes of the slice: x: 2, y: 2, z: 4, core: 2. Of those that a mesh axis runs over, the one named last changes fastest.
Arguments:
- q_rows: bfloat16 [4096, 8192], P(('ctx', 'ch')), may hold values from -6 to 6
- k_rows: bfloat16 [4096, 8192], P(('ctx', 'ch')), may hold values from -6 to 6
- v_rows: bfloat16 [4096, 8192], P(('ctx', 'ch')), may hold values from -6 to 6
- short_taps: float32 [3, 3, 8192], replicated, may hold values from -3.5 to 3.5
- rates: float32 [512, 16], replicated, as said below
- freqs: float32 [512, 16], replicated, may hold values from 0 to 0.05
- residues: float32 [2, 512, 16], replicated, as said below
- skip: float32 [8192], replicated, may hold values from 0.5 to 1.5
Outputs:
- mixed: bfloat16 [4096, 8192], P(('ctx', 'ch'))
Inputs may be any that keep to these rules, and one draw needn't show every extreme that they name: Positive decay rates. Real and imaginary residues of order a few tenths.
All inputs are finite; a program needn't handle non-finite values.
Results may differ from a plain program's by a relative error of at most 0.0058.
Values may be sent and summed in bfloat16 or wider, within the bound.
A program may use at most 192 MiB of HBM per device.

v0:
```python
import math

import jax
import jax.numpy as jnp
from jax import lax
from jax.sharding import PartitionSpec as P

GROUP_WIDTH = 16
MODES = 16


HIGH = lax.Precision.HIGHEST


def passed_along(x, axis, by):
    size = lax.axis_size(axis)
    pairs = [(i, i + by) for i in range(size) if 0 <= i + by < size]
    return lax.ppermute(x, axis, pairs)


def featurize(rows, prior, taps):
    padded = jnp.concatenate([prior, rows], axis=0).astype(jnp.float32)
    return taps[0] * padded[2:] + taps[1] * padded[1:-1] + taps[2] * padded[:-2]


def filter_taps(rates, freqs, residues, length):
    times = jnp.arange(length).astype(jnp.float32)
    decay = jnp.exp(-rates[:, :, None] * times[None, None])
    angle = freqs[:, :, None] * times[None, None]
    terms = decay * (
        residues[0][:, :, None] * jnp.cos(angle) - residues[1][:, :, None] * jnp.sin(angle)
    )
    return jnp.sum(terms, axis=1)


def modal_power(decay_rate, angle_rate, steps):
    amplitude = jnp.exp(-decay_rate * steps)
    return jnp.stack(
        [amplitude * jnp.cos(angle_rate * steps), amplitude * jnp.sin(angle_rate * steps)]
    )


def advance(power, state):
    real = power[0] * state[0] - power[1] * state[1]
    imag = power[0] * state[1] + power[1] * state[0]
    return jnp.stack([real, imag])


def toeplitz(taps):
    span, length = taps.shape
    padded = jnp.concatenate([taps, jnp.zeros((span, length), taps.dtype)], axis=1)
    tiled = jnp.tile(padded, (1, length + 1))[:, : length * (2 * length + 1)]
    shifted = tiled.reshape(span, length, 2 * length + 1)
    return shifted[:, :, length + 1 :][:, :, ::-1]


def local_part(taps, blocked):
    groups = taps.shape[0]
    blocks, half = (blocked.shape[0], blocked.shape[1])
    span = math.gcd(groups, 64)
    count = groups // span
    columns = (
        blocked.astype(jnp.bfloat16)
        .transpose(2, 1, 0, 3)
        .reshape(groups, half, blocks * GROUP_WIDTH)
    )

    def group_block(index):
        matrix = toeplitz(lax.dynamic_slice_in_dim(taps, index * span, span, 0))
        high_part = matrix.astype(jnp.bfloat16)
        low_part = (matrix - high_part.astype(jnp.float32)).astype(jnp.bfloat16)
        inputs = lax.dynamic_slice_in_dim(columns, index * span, span, 0)
        first_term = jnp.einsum(
            "gts,gsn->gtn", high_part, inputs, preferred_element_type=jnp.float32
        )
        second_term = jnp.einsum(
            "gts,gsn->gtn", low_part, inputs, preferred_element_type=jnp.float32
        )
        return first_term + second_term

    results = lax.map(group_block, jnp.arange(count, dtype=jnp.int32))
    return results.reshape(groups, half, blocks, GROUP_WIDTH).transpose(2, 1, 0, 3)


def long_conv(signal_rows, decay_rate, angle_rate, residues, gain, carry_in):
    length, width = signal_rows.shape
    groups = width // GROUP_WIDTH
    half = math.gcd(length, 128)
    blocks = length // half
    signal = signal_rows.astype(jnp.float32)
    blocked = signal.reshape(blocks, half, groups, GROUP_WIDTH)
    chan_decay = jnp.repeat(decay_rate, GROUP_WIDTH, axis=0).T
    chan_angle = jnp.repeat(angle_rate, GROUP_WIDTH, axis=0).T
    block_power = modal_power(chan_decay, chan_angle, float(half))
    tract_power = modal_power(chan_decay, chan_angle, float(length))
    offsets = jnp.arange(half).astype(jnp.float32)
    distance = half - 1.0 - offsets
    amplitude = jnp.exp(-decay_rate[:, :, None] * distance[None, None])
    phase = angle_rate[:, :, None] * distance[None, None]
    reader = jnp.concatenate([amplitude * jnp.cos(phase), amplitude * jnp.sin(phase)], axis=1)
    block_states = jnp.einsum("gks,bsgc->bgkc", reader, blocked, precision=HIGH)
    states = (
        block_states.reshape(blocks, groups, 2, MODES, GROUP_WIDTH)
        .transpose(0, 2, 3, 1, 4)
        .reshape(blocks, 2, MODES, width)
    )

    def run_block(state, entry):
        return (advance(block_power, state) + entry, state)

    own_state, earlier = lax.scan(run_block, jnp.zeros((2, MODES, width), jnp.float32), states)
    incoming = carry_in(tract_power, own_state)
    block_steps = (jnp.arange(blocks) * half).astype(jnp.float32)[:, None, None]
    lifted = advance(modal_power(chan_decay[None], chan_angle[None], block_steps), incoming)
    before_all = earlier + lifted.transpose(1, 0, 2, 3)
    before = (
        before_all.reshape(blocks, 2, MODES, groups, GROUP_WIDTH)
        .transpose(0, 3, 1, 2, 4)
        .reshape(blocks, groups, 2 * MODES, GROUP_WIDTH)
    )
    steps = offsets + 1.0
    amplitude_out = jnp.exp(-decay_rate[:, None, :] * steps[None, :, None])
    phase_out = angle_rate[:, None, :] * steps[None, :, None]
    cosine, sine = (jnp.cos(phase_out), jnp.sin(phase_out))
    real = amplitude_out * (residues[0][:, None, :] * cosine - residues[1][:, None, :] * sine)
    imag = amplitude_out * (residues[0][:, None, :] * sine + residues[1][:, None, :] * cosine)
    writer = jnp.concatenate([real, -imag], axis=2)
    carried = jnp.einsum("gtk,bgkc->btgc", writer, before, precision=HIGH)
    local = local_part(filter_taps(decay_rate, angle_rate, residues, half), blocked)
    total = local + carried + gain.reshape(groups, GROUP_WIDTH) * blocked
    return total.reshape(length, width)


def context_carry(state, chan_decay, chan_angle, stretch):
    tract_index = lax.axis_index("ctx")
    piece = lax.all_gather(state[None], "ctx", axis=0, tiled=True)
    count = piece.shape[0]
    index = jnp.arange(count, dtype=jnp.int32)
    distance = (tract_index - 1 - index).astype(jnp.float32)
    valid = (distance >= 0.0).astype(jnp.float32)[:, None, None]
    steps = (jnp.maximum(distance, 0.0) * float(stretch))[:, None, None]
    amplitude = jnp.exp(-chan_decay[None] * steps) * valid
    cosine = amplitude * jnp.cos(chan_angle[None] * steps)
    sine = amplitude * jnp.sin(chan_angle[None] * steps)
    real = jnp.sum(cosine * piece[:, 0] - sine * piece[:, 1], axis=0)
    imag = jnp.sum(cosine * piece[:, 1] + sine * piece[:, 0], axis=0)
    return jnp.stack([real, imag])


def body(q_rows, k_rows, v_rows, short_taps, rates, freqs, residues, skip):
    prior_tails = passed_along((q_rows[-2:], k_rows[-2:], v_rows[-2:]), ("ctx", "ch"), 1)
    q_feat = featurize(q_rows, prior_tails[0], short_taps[0])
    k_feat = featurize(k_rows, prior_tails[1], short_taps[1])
    v_feat = featurize(v_rows, prior_tails[2], short_taps[2])
    gated_rows = (k_feat * v_feat).astype(jnp.bfloat16)
    members = lax.axis_size("ch")
    share_width = q_rows.shape[1] // members
    share_groups = share_width // GROUP_WIDTH
    first = lax.axis_index("ch") * share_groups
    decay_rate = lax.dynamic_slice_in_dim(rates, first, share_groups, 0)
    angle_rate = lax.dynamic_slice_in_dim(freqs, first, share_groups, 0)
    chan_decay = jnp.repeat(decay_rate, GROUP_WIDTH, axis=0).T
    chan_angle = jnp.repeat(angle_rate, GROUP_WIDTH, axis=0).T
    stretch = q_rows.shape[0] * members
    tract_rows = lax.all_to_all(gated_rows, "ch", split_axis=1, concat_axis=0, tiled=True)
    local_residues = lax.dynamic_slice_in_dim(residues, first, share_groups, 1)
    gain = lax.dynamic_slice_in_dim(skip, lax.axis_index("ch") * share_width, share_width, 0)

    def grid_carry(power, state):
        return context_carry(state, chan_decay, chan_angle, stretch)

    conv = long_conv(tract_rows, decay_rate, angle_rate, local_residues, gain, grid_carry).astype(
        jnp.bfloat16
    )
    conv_rows = lax.all_to_all(conv, "ch", split_axis=0, concat_axis=1, tiled=True)
    return (q_feat * conv_rows.astype(jnp.float32)).astype(jnp.bfloat16)


def solution(mesh):
    placed = (
        P(("ctx", "ch"), None),
        P(("ctx", "ch"), None),
        P(("ctx", "ch"), None),
        P(),
        P(),
        P(),
        P(),
        P(),
    )
    return jax.shard_map(
        body, mesh=mesh, in_specs=placed, out_specs=P(("ctx", "ch"), None), check_vma=False
    )
```

profile of v0, /device:TPU:12, one launch (start us, length us, event | category | flops | bytes accessed | tf_op | source)
XLA Modules:
  0.0 337.6 jit_solution(3373065804913915332)
XLA Ops:
  31.8 9.7 %fusion.50 = (f32[128,16,128]{2,1,0:T(8,128)S(1)}, f32[128,16,128]{2,1,0:T(8,128)}, f32[128,128]{1,0:T(8,128)S(1)}) fusion(f32[128]{0:T(128)S(1)} %broadcast_subtract_fusion, f32[128,16]{1,0:T(8,128)S(1)} %copy.59, f32[128,16]{1,0:T(8,128)} %copy.57, f32[128,16]{1,0:T(8,128)} %copy.60, f32[128,16]{1,0:T(8,128)} %copy.58, f32[128]{0:T(128)S(1)} %iota_convert_fusion), kind=kLoop, calls=%fused_computation.84 | loop fusion | flops 2867200 | bytes 2196480 | tf_op jit(solution)/shard_map/mul | solution.py:100
  41.5 12.0 %all-to-all-done = bf16[128,4,2048]{0,2,1:T(8,128)(2,1)S(1)} async-done(((bf16[128,4,2048]{0,2,1:T(8,128)(2,1)}), bf16[128,4,2048]{0,2,1:T(8,128)(2,1)S(1)}, u32[]{:S(2)}, u32[]{:S(2)}) %all-to-all-start) | async-done | bytes 2097184 | tf_op jit(solution)/shard_map/all_to_all | solution.py:165
  53.4 6.8 %convolution_bitcast_fusion = f32[4,128,32,16]{2,3,0,1:T(8,128)} fusion(f32[128,16,128]{2,1,0:T(8,128)} %get-tuple-element.183, f32[128,16,128]{2,1,0:T(8,128)S(1)} %get-tuple-element.182, bf16[4,128,128,16]{1,3,2,0:T(8,128)(2,1)S(1)} %bitcast.164), kind=kOutput, calls=%fused_computation.54 | convolution fusion | flops 403177472 | bytes 5242880 | tf_op jit(solution)/shard_map/gks,bsgc->bgkc/dot_general | solution.py:101
  60.3 9.0 %copy.78 = f32[4,128,32,16]{3,1,2,0:T(8,128)} copy(f32[4,128,32,16]{2,3,0,1:T(8,128)} %convolution_bitcast_fusion) | data formatting | bytes 2097152 | tf_op jit(solution)/shard_map/transpose | solution.py:104
  69.3 7.9 %reshape.167 = f32[4,2,16,2048]{3,2,1,0:T(8,128)S(1)} reshape(f32[4,2,16,128,16]{4,3,2,1,0:T(8,128)} %bitcast.162) | data formatting | bytes 2097152 | tf_op jit(solution)/shard_map/reshape | solution.py:105
  77.2 13.0 %while.26 = (s32[]{:T(128)}, f32[2,16,2048]{2,1,0:T(8,128)S(1)}, f32[4,2,16,2048]{3,2,1,0:T(8,128)}, f32[4,2,16,2048]{3,2,1,0:T(8,128)S(1)}, f32[128,16]{0,1:T(8...) while((s32[]{:T(128)}, f32[2,16,2048]{2,1,0:T(8,128)S(1)}, ...), condition=%wide.region_4.5_spmd.clone.clone.clone, body=%wide.region_3.4_spmd.clone.clone.clone.sunk | while | flops 524291 | bytes 3162223 | solution.py:111
  93.8 5.8 %fusion.41 = (f32[128,128,16]{1,2,0:T(8,128)}, f32[128,128,16]{1,2,0:T(8,128)}) fusion(f32[128,16]{1,0:T(8,128)S(1)} %copy-done.6, f32[128,16]{1,0:T(8,128)S(1)} %copy.59, f32[128,16]{1,0:T(8,128)S(1)} %copy-done.7, f32[128]{0:T(128)S(1)} %broadcast_add_fusion, f32[128,16]{1,0:T(8,128)S(1)} %copy-done.5), kind=kLoop, calls=%fused_computation.75 | loop fusion | flops 2883584 | bytes 2130432 | tf_op jit(solution)/shard_map/mul | solution.py:125
  101.9 139.5 %while.25 = (s32[]{:T(128)}, f32[2,64,128,64]{2,3,1,0:T(8,128)}, s32[2]{0:T(128)S(1)}, f32[128,128]{1,0:T(8,128)S(1)}, bf16[128,128,64]{1,2,0:T(8,128)(2,1)S(1)}...) while((s32[]{:T(128)}, f32[2,64,128,64]{2,3,1,0:T(8,128)}, s32[2]{0:T(128)S(1)}, ...), condition=%wide.region_2.3_spmd, body=%wide.region_1.2_spmd.sunk | while | flops 274202624 | bytes 109609176 | solution.py:81
  110.3 14.3 %reshape.194 = f32[64,128,257]{2,1,0:T(8,128)} reshape(f32[64,32896]{1,0:T(8,128)} %slice.232) | data formatting | bytes 16842752 | tf_op jit(solution)/shard_map/while/body/eval_jaxpr/reshape | solution.py:53
  124.6 6.5 %slice.233 = f32[64,128,128]{2,1,0:T(8,128)} slice(f32[64,128,257]{2,1,0:T(8,128)} %reshape.194), slice={[0:64], [0:128], [129:257]} | slice | bytes 8388608 | tf_op jit(solution)/shard_map/while/body/eval_jaxpr/slice | solution.py:54
  131.1 33.9 %rev.4 = f32[64,128,128]{2,1,0:T(8,128)} reverse(f32[64,128,128]{2,1,0:T(8,128)} %slice.233), dimensions={2} | reverse | bytes 8388608 | tf_op jit(solution)/shard_map/while/body/eval_jaxpr/rev | solution.py:54
  165.0 3.9 %fusion.68 = f32[64,128,64]{1,2,0:T(8,128)S(1)} fusion(f32[64,128,128]{2,1,0:T(8,128)} %rev.4, bf16[128,128,64]{1,2,0:T(8,128)(2,1)S(1)} %get-tuple-element.289, s32[]{:T(128)S(6)} %select_n.15), kind=kOutput, calls=%fused_computation.6.clone.1 | convolution fusion | flops 135266304 | bytes 7340036 | tf_op jit(solution)/shard_map/while/body/eval_jaxpr/gts,gsn->gtn/dot_general | solution.py:73
  176.2 3.7 %slice.232 = f32[64,32896]{1,0:T(8,128)} slice(f32[64,33024]{1,0:T(8,128)S(1)} %bitcast.160), slice={[0:64], [0:32896]} | slice | bytes 16842752 | tf_op jit(solution)/shard_map/while/body/eval_jaxpr/slice | solution.py:52
  180.0 14.2 %reshape.194 = f32[64,128,257]{2,1,0:T(8,128)} reshape(f32[64,32896]{1,0:T(8,128)} %slice.232) | data formatting | bytes 16842752 | tf_op jit(solution)/shard_map/while/body/eval_jaxpr/reshape | solution.py:53
  194.2 6.5 %slice.233 = f32[64,128,128]{2,1,0:T(8,128)} slice(f32[64,128,257]{2,1,0:T(8,128)} %reshape.194), slice={[0:64], [0:128], [129:257]} | slice | bytes 8388608 | tf_op jit(solution)/shard_map/while/body/eval_jaxpr/slice | solution.py:54
  200.6 33.9 %rev.4 = f32[64,128,128]{2,1,0:T(8,128)} reverse(f32[64,128,128]{2,1,0:T(8,128)} %slice.233), dimensions={2} | reverse | bytes 8388608 | tf_op jit(solution)/shard_map/while/body/eval_jaxpr/rev | solution.py:54
  234.6 3.9 %fusion.68 = f32[64,128,64]{1,2,0:T(8,128)S(1)} fusion(f32[64,128,128]{2,1,0:T(8,128)} %rev.4, bf16[128,128,64]{1,2,0:T(8,128)(2,1)S(1)} %get-tuple-element.289, s32[]{:T(128)S(6)} %select_n.15), kind=kOutput, calls=%fused_computation.6.clone.1 | convolution fusion | flops 135266304 | bytes 7340036 | tf_op jit(solution)/shard_map/while/body/eval_jaxpr/gts,gsn->gtn/dot_general | solution.py:73
  241.4 7.0 %subtract_reduce_fusion = (f32[16,2048]{1,0:T(8,128)S(1)}, f32[16,2048]{1,0:T(8,128)S(1)}) fusion(f32[8,2,16,2048]{3,2,1,0:T(8,128)} %bitcast.171, f32[16,2048]{1,0:T(8,128)S(1)} %bitcast.172, f32[8]{0:T(128)S(1)} %compare_convert_fusion, f32[8]{0:T(128)S(1)} %maximum_multiply_fusion, f32[16,2048]{1,0:T(8,128)S(1)} %bitcast.174), kind=kLoop, calls=%fused_computation.94 | loop fusion | flops 3342336 | bytes 2621504 | tf_op jit(solution)/shard_map/reduce_sum | solution.py:145
  251.9 4.9 %reshape.168 = f32[4,2,16,128,16]{4,3,2,1,0:T(8,128)} reshape(f32[4,2,16,2048]{3,2,1,0:T(8,128)S(1)} %fusion.54) | data formatting | bytes 2097152 | tf_op jit(solution)/shard_map/reshape | solution.py:117
  256.8 22.5 %fusion.28 = bf16[4,128,128,16]{1,3,0,2:T(8,128)(2,1)S(1)} fusion(f32[4,128,128,16]{1,3,0,2:T(8,128)} %bitcast.170, f32[4,128,32,16]{3,1,2,0:T(8,128)} %bitcast.163, f32[128,128,16]{1,2,0:T(8,128)} %get-tuple-element.181, f32[128,128,16]{1,2,0:T(8,128)} %get-tuple-element.180, f32[128,16]{1,0:T(8,128)S(1)} %mul.589, bf16[4,128,128,16]{1,3,2,0:T(8,128)(2,1)S(1)} %bitcast.166), kind=kOutput, calls=%fused_computation.50 | convolution fusion | flops 408420352 | bytes 11542528 | tf_op jit(solution)/shard_map/gtk,bgkc->btgc/dot_general | solution.py:128
  287.9 22.4 %collective-permute-done = bf16[2,8192]{1,0:T(2,128)(2,1)S(1)} collective-permute-done((bf16[2,8192]{1,0:T(2,128)(2,1)S(1)}, bf16[2,8192]{1,0:T(2,128)(2,1)S(1)}, u32[]{:S(2)}, u32[]{:S(2)}) %collective-permute-start) | collective-permute-done | bytes 32800 | tf_op jit(solution)/shard_map/ppermute | solution.py:18
  310.3 4.3 %maximum_convert_fusion = f32[130,8192]{1,0:T(8,128)} fusion(bf16[128,8192]{1,0:T(8,128)(2,1)} %param.12, bf16[2,8192]{1,0:T(2,128)(2,1)S(1)} %collective-permute-done), kind=kLoop, calls=%fused_computation.51 | loop fusion | flops 4259840 | bytes 6389760 | tf_op jit(solution)/shard_map/convert_element_type | solution.py:22
  316.8 5.7 %copy.75 = f32[128,8192]{1,0:T(8,128)} copy(f32[128,8192]{0,1:T(8,128)} %bitcast.167) | data formatting | bytes 8388608 | tf_op jit(solution)/shard_map/convert_element_type | solution.py:176
  322.5 8.2 %fusion.25 = bf16[128,8192]{1,0:T(8,128)(2,1)} fusion(f32[128,8192]{1,0:T(8,128)} %copy.75, f32[130,8192]{1,0:T(8,128)} %maximum_convert_fusion, f32[8192]{0:T(1024)S(1)} %bitcast.177, f32[8192]{0:T(1024)S(1)} %bitcast.178, f32[8192]{0:T(1024)S(1)} %bitcast.176), kind=kLoop, calls=%fused_computation.44 | loop fusion | flops 7340032 | bytes 18972672 | tf_op jit(solution)/shard_map/convert_element_type | solution.py:176
  (111 shorter events, 75.2 us)
Async XLA Ops:
  6.5 11.9 %copy-start.4 = (bf16[128,8192]{1,0:T(8,128)(2,1)S(1)}, bf16[128,8192]{1,0:T(8,128)(2,1)}, u32[]{:S(2)}) copy-start(bf16[128,8192]{1,0:T(8,128)(2,1)} %param.13) | copy-start | bytes 6291460
  7.6 8.6 %collective-permute-start.2 = (bf16[2,8192]{1,0:T(2,128)(2,1)S(1)}, bf16[2,8192]{1,0:T(2,128)(2,1)S(1)}, u32[]{:S(2)}, u32[]{:S(2)}) collective-permute-start(bf16[2,8192]{1,0:T(2,128)(2,1)S(1)} %slice.133), channel_id=1, source_target_pairs={{0,1},{1,2},{2,3},{3,4},{4,5},{5,6},{6,7},{7,8},{8,9},{9,10},{10,1... | collective-permute-start | bytes 98312 | tf_op jit(solution)/shard_map/ppermute | solution.py:18
  10.5 7.9 %collective-permute-start.1 = (bf16[2,8192]{1,0:T(2,128)(2,1)S(1)}, bf16[2,8192]{1,0:T(2,128)(2,1)S(1)}, u32[]{:S(2)}, u32[]{:S(2)}) collective-permute-start(bf16[2,8192]{1,0:T(2,128)(2,1)S(1)} %slice.126), channel_id=1, source_target_pairs={{0,1},{1,2},{2,3},{3,4},{4,5},{5,6},{6,7},{7,8},{8,9},{9,10},{10,1... | collective-permute-start | bytes 98312 | tf_op jit(solution)/shard_map/ppermute | solution.py:18
  24.2 29.2 %all-to-all-start = ((bf16[128,4,2048]{0,2,1:T(8,128)(2,1)}), bf16[128,4,2048]{0,2,1:T(8,128)(2,1)S(1)}, u32[]{:S(2)}, u32[]{:S(2)}) async-start(bf16[128,4,2048]{0,2,1:T(8,128)(2,1)} %bitcast.168), calls=%async_computation | async-start | bytes 4194304 | tf_op jit(solution)/shard_map/all_to_all | solution.py:165
  27.8 213.6 %all-gather.3.cloned.1.call-start = ((), (), s32[]{:S(2)}) async-start(), calls=%async_computation.2 | async-start | bytes 2359296 | tf_op jit(solution)/shard_map/all_gather | solution.py:136
  53.4 6.8 %copy-start.1 = (bf16[128,4,2048]{0,2,1:T(8,128)(2,1)}, bf16[128,4,2048]{0,2,1:T(8,128)(2,1)S(1)}, u32[]{:S(2)}) copy-start(bf16[128,4,2048]{0,2,1:T(8,128)(2,1)S(1)} %all-to-all-done) | copy-start | bytes 6291460
  90.2 0.7 copy-start.3
  90.2 3.5 %copy-start.5 = (f32[128,16]{1,0:T(8,128)S(1)}, f32[128,16]{1,0:T(8,128)}, u32[]{:S(2)}) copy-start(f32[128,16]{1,0:T(8,128)} %copy.57) | copy-start | bytes 24580
  90.2 3.5 %copy-start.6 = (f32[128,16]{1,0:T(8,128)S(1)}, f32[128,16]{1,0:T(8,128)}, u32[]{:S(2)}) copy-start(f32[128,16]{1,0:T(8,128)} %copy.60) | copy-start | bytes 24580
  90.2 3.5 %copy-start.7 = (f32[128,16]{1,0:T(8,128)S(1)}, f32[128,16]{1,0:T(8,128)}, u32[]{:S(2)}) copy-start(f32[128,16]{1,0:T(8,128)} %copy.58) | copy-start | bytes 24580
  165.0 3.9 %copy-start = (f32[64,128,128]{2,1,0:T(8,128)S(1)}, f32[64,128,128]{2,1,0:T(8,128)}, u32[]{:S(2)}) copy-start(f32[64,128,128]{2,1,0:T(8,128)} %rev.4) | copy-start | bytes 12582916 | tf_op jit(solution)/shard_map/while
  234.6 3.9 %copy-start = (f32[64,128,128]{2,1,0:T(8,128)S(1)}, f32[64,128,128]{2,1,0:T(8,128)}, u32[]{:S(2)}) copy-start(f32[64,128,128]{2,1,0:T(8,128)} %rev.4) | copy-start | bytes 12582916 | tf_op jit(solution)/shard_map/while
  251.9 4.9 %copy-start.2 = (bf16[128,4,2048]{0,2,1:T(8,128)(2,1)S(1)}, bf16[128,4,2048]{0,2,1:T(8,128)(2,1)}, u32[]{:S(2)}) copy-start(bf16[128,4,2048]{0,2,1:T(8,128)(2,1)} %copy-done.1) | copy-start | bytes 6291460
  281.0 33.6 %all-to-all-start.1 = ((bf16[4,128,2048]{1,2,0:T(8,128)(2,1)}), bf16[4,128,2048]{1,2,0:T(8,128)(2,1)S(1)}, u32[]{:S(2)}, u32[]{:S(2)}) async-start(bf16[4,128,2048]{1,2,0:T(8,128)(2,1)} %bitcast.169), calls=%async_computation.1 | async-start | bytes 4194304 | tf_op jit(solution)/shard_map/all_to_all | solution.py:175
  285.5 24.8 %collective-permute-start = (bf16[2,8192]{1,0:T(2,128)(2,1)S(1)}, bf16[2,8192]{1,0:T(2,128)(2,1)S(1)}, u32[]{:S(2)}, u32[]{:S(2)}) collective-permute-start(bf16[2,8192]{1,0:T(2,128)(2,1)S(1)} %slice.117), channel_id=1, source_target_pairs={{0,1},{1,2},{2,3},{3,4},{4,5},{5,6},{6,7},{7,8},{8,9},{9,10},{10,1... | collective-permute-start | bytes 98312 | tf_op jit(solution)/shard_map/ppermute | solution.py:18
  316.8 5.7 %copy-start.8 = (f32[1,1,8192]{2,1,0:T(1,128)S(1)}, f32[1,1,8192]{2,1,0:T(1,128)}, u32[]{:S(2)}) copy-start(f32[1,1,8192]{2,1,0:T(1,128)} %get-tuple-element.171) | copy-start | bytes 98308
  316.8 5.7 %copy-start.9 = (f32[1,1,8192]{2,1,0:T(1,128)S(1)}, f32[1,1,8192]{2,1,0:T(1,128)}, u32[]{:S(2)}) copy-start(f32[1,1,8192]{2,1,0:T(1,128)} %get-tuple-element.176) | copy-start | bytes 98308
  316.8 5.7 %copy-start.10 = (f32[1,1,8192]{2,1,0:T(1,128)S(1)}, f32[1,1,8192]{2,1,0:T(1,128)}, u32[]{:S(2)}) copy-start(f32[1,1,8192]{2,1,0:T(1,128)} %get-tuple-element.177) | copy-start | bytes 98308
Sparse Core Ops, SparseCore 0:
  91.1 48.3 all-gather.2
where the time goes:
time: 344 us; the launch traced here: 338 us
  local copies, waits for them, and re-layouts  177 us (51%)
  other arithmetic  52.1 us (15%)
  matrix products  43 us (12%)
  waiting for transfers between devices  34.4 us (10%)
  starting transfers between devices  15.2 us (4%)
  between operations  13.7 us (4%)
    rev x2, local copies, waits for them, and re-layouts, toeplitz(): return shifted[:, :, length + 1:][:, :, ::-1]  67.9 us
    reshape x2, local copies, waits for them, and re-layouts, toeplitz(): shifted = tiled.reshape(span, length, 2 * length + 1)  28.5 us
    dot_general x1, matrix products, long_conv(): carried = jnp.einsum('gtk,bgkc->btgc', writer, before, precision=HIGH)  22.5 us
    ppermute x3, waiting for transfers between devices, passed_along(): return lax.ppermute(x, axis, pairs)  22.4 us
    slice x2, local copies, waits for them, and re-layouts, toeplitz(): return shifted[:, :, length + 1:][:, :, ::-1]  13 us
    all_to_all x1, waiting for transfers between devices, body(): lax.all_to_all(gated_rows, 'ch', split_axis=1, concat_axis=0, tiled=True)  12 us
    convert_element_type x2, other arithmetic, body(): return (q_feat * conv_rows.astype(jnp.float32)).astype(jnp.bfloat16)  10.5 us
    mul x1, other arithmetic, long_conv(): amplitude * jnp.cos(phase)  9.69 us
  transfers between devices with their start and end apart: 6, of which 2 were waited for; matrix products, arithmetic and copies ran while one was open for 51% of the time, Pallas kernels for 0%

commit v1 on v0

v1 whole, which is shorter than its diff:
```python
import jax
import jax.numpy as jnp
from jax import lax
from jax.experimental import pallas as pl
from jax.experimental.pallas import tpu as pltpu
from jax.sharding import PartitionSpec as P

GROUP_WIDTH = 16
MODES = 16
HALF = 128
LANES = 128
PACK = LANES // GROUP_WIDTH
STATE = 2 * MODES


def complex_power(decay, angle, steps):
    amplitude = jnp.exp(-decay * steps)
    return amplitude * jnp.cos(angle * steps), amplitude * jnp.sin(angle * steps)


def mode_table(decay, angle, coef, coarse, fine):
    hr, hi = complex_power(decay[None], angle[None], coarse[:, None])
    hr, hi = coef[0] * hr - coef[1] * hi, coef[0] * hi + coef[1] * hr
    lr, li = complex_power(decay[None], angle[None], fine[:, None])
    full = hr[:, None] * lr[None] - hi[:, None] * li[None]
    return full.reshape(coarse.shape[0] * fine.shape[0], -1).astype(jnp.bfloat16)


def shifted(rows, prior, by):
    moved = pltpu.roll(rows, by, 0)
    index = lax.broadcasted_iota(jnp.int32, rows.shape, 0)
    for row in range(by):
        moved = jnp.where(index == row, prior[2 - by + row : 3 - by + row], moved)
    return moved


def featurize(rows_ref, prior, taps):
    rows = rows_ref[...].astype(jnp.float32)
    return (
        taps[0:1] * rows
        + taps[1:2] * shifted(rows, prior, 1)
        + taps[2:3] * shifted(rows, prior, 2)
    )


def gate_kernel(k_ref, v_ref, prior_ref, taps_ref, out_ref):
    prior = prior_ref[...].astype(jnp.float32)
    k_feat = featurize(k_ref, prior[2:4], taps_ref[1])
    v_feat = featurize(v_ref, prior[4:6], taps_ref[2])
    out_ref[0] = (k_feat * v_feat).astype(jnp.bfloat16)


def mix_kernel(q_ref, prior_ref, taps_ref, conv_ref, out_ref):
    prior = prior_ref[...].astype(jnp.float32)
    q_feat = featurize(q_ref, prior[0:2], taps_ref[0])
    out_ref[...] = (q_feat * conv_ref[0].astype(jnp.float32)).astype(jnp.bfloat16)


def advance(power, state):
    pr, pi = power[:MODES], power[MODES:]
    sr, si = state[:MODES], state[MODES:]
    return jnp.concatenate([pr * sr - pi * si, pr * si + pi * sr], axis=0)


def own_group(rows):
    shape = (PACK * rows, LANES)
    row = lax.broadcasted_iota(jnp.int32, shape, 0) // rows
    lane = lax.broadcasted_iota(jnp.int32, shape, 1) // GROUP_WIDTH
    return row == lane


def summary_kernel(x_ref, reader_ref, power_ref, earlier_ref, own_ref):
    blocks = x_ref.shape[0] // HALF
    mask = own_group(STATE)
    reader = reader_ref[...]
    power = power_ref[...]
    state = jnp.zeros((STATE, LANES), jnp.float32)
    for block in range(blocks):
        rows = x_ref[block * HALF : (block + 1) * HALF, :]
        full = lax.dot_general(
            reader, rows, (((0,), (0,)), ((), ())), preferred_element_type=jnp.float32
        )
        entry = jnp.where(mask, full, 0.0).reshape(PACK, STATE, LANES).sum(axis=0)
        earlier_ref[block * STATE : (block + 1) * STATE, :] = state
        state = advance(power, state) + entry
    own_ref[0] = state


def conv_kernel(
    x_ref, taps_ref, writer_ref, earlier_ref, carry_ref, power_ref, gain_ref, out_ref, left, right
):
    blocks = x_ref.shape[0] // HALF
    row = lax.broadcasted_iota(jnp.int32, (HALF, HALF), 0)
    lane = lax.broadcasted_iota(jnp.int32, (HALF, HALF), 1)
    causal = lane <= row
    for group in range(PACK):
        wide = jnp.broadcast_to(taps_ref[group : group + 1, :], (HALF, HALF))
        turned = pltpu.roll(wide, 0, 1, stride=1, stride_axis=0)
        left[:, group * HALF : (group + 1) * HALF] = jnp.where(causal, turned, 0.0).astype(
            jnp.bfloat16
        )
    left[:, PACK * HALF :] = writer_ref[...]
    mask = own_group(STATE)
    lane_group = lane // GROUP_WIDTH
    power = power_ref[...]
    gain = gain_ref[...]
    lifted = carry_ref[0]
    for block in range(blocks):
        cols = slice(block * LANES, (block + 1) * LANES)
        rows = x_ref[block * HALF : (block + 1) * HALF, :].astype(jnp.float32)
        for group in range(PACK):
            right[group * HALF : (group + 1) * HALF, cols] = jnp.where(
                lane_group == group, rows, 0.0
            ).astype(jnp.bfloat16)
        state = earlier_ref[block * STATE : (block + 1) * STATE, :] + lifted
        spread = jnp.where(mask, jnp.concatenate([state] * PACK, axis=0), 0.0)
        right[PACK * HALF :, cols] = spread.astype(jnp.bfloat16)
        lifted = advance(power, lifted)
    step = 2 if blocks % 2 == 0 else 1
    for first in range(0, blocks, step):
        total = jnp.dot(
            left[...],
            right[:, first * LANES : (first + step) * LANES],
            preferred_element_type=jnp.float32,
        )
        for inner in range(step):
            span = slice((first + inner) * HALF, (first + inner + 1) * HALF)
            part = total[:, inner * LANES : (inner + 1) * LANES]
            out_ref[span, :] = (part + gain * x_ref[span, :].astype(jnp.float32)).astype(
                jnp.bfloat16
            )


def body(q_rows, k_rows, v_rows, short_taps, rates, freqs, residues, skip):
    members = lax.axis_size("ch")
    tracts = lax.axis_size("ctx")
    size = members * tracts
    count, width = q_rows.shape
    share = width // members
    share_groups = share // GROUP_WIDTH
    length = count * members
    blocks = length // HALF
    lane_blocks = share // LANES
    me = lax.axis_index("ch")

    tails = jnp.concatenate([q_rows[-2:], k_rows[-2:], v_rows[-2:]], axis=0)
    prior = lax.ppermute(tails, ("ctx", "ch"), [(i, i + 1) for i in range(size - 1)])

    tile = 1024
    per = share // tile
    rows_spec = pl.BlockSpec((count, tile), lambda j: (0, j))
    prior_spec = pl.BlockSpec((6, tile), lambda j: (0, j))
    taps_spec = pl.BlockSpec((3, 3, tile), lambda j: (0, 0, j))
    split_spec = pl.BlockSpec((1, count, tile), lambda j: (j // per, 0, j % per))
    gated = pl.pallas_call(
        gate_kernel,
        grid=(width // tile,),
        in_specs=[rows_spec, rows_spec, prior_spec, taps_spec],
        out_specs=split_spec,
        out_shape=jax.ShapeDtypeStruct((members, count, share), jnp.bfloat16),
        cost_estimate=pl.CostEstimate(
            flops=12 * count * width, bytes_accessed=6 * count * width, transcendentals=0
        ),
    )(k_rows, v_rows, prior, short_taps)
    signal = lax.all_to_all(gated, "ch", split_axis=0, concat_axis=0).reshape(length, share)

    first = me * share_groups
    decay = lax.dynamic_slice_in_dim(rates, first, share_groups, 0)
    angle = lax.dynamic_slice_in_dim(freqs, first, share_groups, 0)
    res = lax.dynamic_slice_in_dim(residues, first, share_groups, 1)
    gain = lax.dynamic_slice_in_dim(skip, me * share, share, 0)[None]
    decay2 = jnp.concatenate([decay, decay], axis=1).reshape(-1)
    angle2 = jnp.concatenate([angle, angle], axis=1).reshape(-1)
    ones, zeros = jnp.ones_like(decay), jnp.zeros_like(decay)
    read_coef = (
        jnp.concatenate([ones, zeros], axis=1).reshape(-1),
        jnp.concatenate([zeros, -ones], axis=1).reshape(-1),
    )
    write_coef = (
        jnp.concatenate([res[0], -res[1]], axis=1).reshape(-1),
        jnp.concatenate([res[1], res[0]], axis=1).reshape(-1),
    )
    coarse = jnp.arange(HALF // 16).astype(jnp.float32) * 16.0
    fine = jnp.arange(16).astype(jnp.float32)
    reader = mode_table(decay2, angle2, read_coef, coarse[::-1], fine[::-1])
    writer = mode_table(decay2, angle2, write_coef, coarse + 1.0, fine)
    back = lax.rem(HALF - jnp.arange(HALF), HALF).astype(jnp.float32)[None, None]
    tap_re, tap_im = complex_power(decay[:, :, None], angle[:, :, None], back)
    taps = jnp.sum(res[0][:, :, None] * tap_re - res[1][:, :, None] * tap_im, axis=1)
    chan_decay = jnp.repeat(decay.T, GROUP_WIDTH, axis=1)
    chan_angle = jnp.repeat(angle.T, GROUP_WIDTH, axis=1)
    power = jnp.concatenate(complex_power(chan_decay, chan_angle, float(HALF)), axis=0)

    piece = share // tracts
    sub = piece // LANES
    signal_spec = pl.BlockSpec((length, LANES), lambda j: (0, j))
    table_spec = pl.BlockSpec((HALF, PACK * STATE), lambda j: (0, j))
    state_spec = pl.BlockSpec((STATE, LANES), lambda j: (0, j))
    earlier_spec = pl.BlockSpec((blocks * STATE, LANES), lambda j: (0, j))
    relay_spec = pl.BlockSpec((1, STATE, LANES), lambda j: (j // sub, 0, j % sub))
    earlier, own = pl.pallas_call(
        summary_kernel,
        grid=(lane_blocks,),
        in_specs=[signal_spec, table_spec, state_spec],
        out_specs=[earlier_spec, relay_spec],
        out_shape=[
            jax.ShapeDtypeStruct((blocks * STATE, share), jnp.float32),
            jax.ShapeDtypeStruct((tracts, STATE, piece), jnp.float32),
        ],
    )(signal, reader, power)

    gathered = lax.all_to_all(own, "ctx", split_axis=0, concat_axis=0)
    mine = lax.axis_index("ctx") * piece
    tract_power = complex_power(
        lax.dynamic_slice_in_dim(chan_decay, mine, piece, 1),
        lax.dynamic_slice_in_dim(chan_angle, mine, piece, 1),
        float(length),
    )
    tract_power = jnp.concatenate(tract_power, axis=0)
    state = jnp.zeros((STATE, piece), jnp.float32)
    incoming = []
    for tract in range(tracts):
        incoming.append(state)
        state = advance(tract_power, state) + gathered[tract]
    carry = lax.all_to_all(jnp.stack(incoming), "ctx", split_axis=0, concat_axis=0)

    conv = pl.pallas_call(
        conv_kernel,
        grid=(lane_blocks,),
        in_specs=[
            signal_spec,
            pl.BlockSpec((PACK, HALF), lambda j: (j, 0)),
            table_spec,
            earlier_spec,
            relay_spec,
            state_spec,
            pl.BlockSpec((1, LANES), lambda j: (0, j)),
        ],
        out_specs=signal_spec,
        out_shape=jax.ShapeDtypeStruct((length, share), jnp.bfloat16),
        scratch_shapes=[
            pltpu.VMEM((HALF, PACK * (HALF + STATE)), jnp.bfloat16),
            pltpu.VMEM((PACK * (HALF + STATE), blocks * LANES), jnp.bfloat16),
        ],
    )(signal, taps, writer, earlier, carry, power, gain)

    conv_rows = lax.all_to_all(
        conv.reshape(members, count, share), "ch", split_axis=0, concat_axis=0
    )
    return pl.pallas_call(
        mix_kernel,
        grid=(width // tile,),
        in_specs=[rows_spec, prior_spec, taps_spec, split_spec],
        out_specs=rows_spec,
        out_shape=jax.ShapeDtypeStruct((count, width), jnp.bfloat16),
    )(q_rows, prior, short_taps, conv_rows)


def solution(mesh):
    rows = P(("ctx", "ch"), None)
    return jax.shard_map(
        body,
        mesh=mesh,
        in_specs=(rows, rows, rows, P(), P(), P(), P(), P()),
        out_specs=rows,
        check_vma=False,
    )
```

time: 344 us -> 153 us (0.44); the launches traced: 338 us -> 150 us
  local copies, waits for them, and re-layouts: 177 us -> 12.5 us
  matrix products: 43 us -> 0 us
  Pallas kernels: 0 us -> 40.7 us
  other arithmetic: 52.1 us -> 20.9 us
  blocking collectives: 0 us -> 30.1 us
  between operations: 13.7 us -> 0.27 us
  waiting for transfers between devices: 34.4 us -> 28.8 us
    rev x2 -> x1, local copies, waits for them, and re-layouts: 67.9 us -> 0.1 us  [body(): reader = mode_table(decay2, angle2, read_coef, coarse[::-1], fine[::-1])]
    reshape x9 -> x2, local copies, waits for them, and re-layouts: 44.3 us -> 1.26 us  [the longest x1 0.63 us: body(): chan_angle = jnp.repeat(angle.T, GROUP_WIDTH, axis=1)]
    dot_general x6 -> x0, matrix products: 43 us -> none  [the longest x1 22.5 us: long_conv(): carried = jnp.einsum('gtk,bgkc->btgc', writer, before, precision=HIGH)]
    pallas_call x0 -> x4, Pallas kernels: none -> 40.7 us  [the longest x1 14.7 us: body(): pl.pallas_call(conv_kernel, grid=(lane_blocks,), in_specs=[signal_spec, p...]
    all_to_all x0 -> x1, blocking collectives: none -> 30.1 us  [body(): lax.all_to_all(conv.reshape(members, count, share), 'ch', split_axis=0, c...]
    slice x8 -> x3, local copies, waits for them, and re-layouts: 25.7 us -> 2.83 us  [body(): tails = jnp.concatenate([q_rows[-2:], k_rows[-2:], v_rows[-2:]], axis=0)]
    ppermute x3 -> x1, waiting for transfers between devices: 22.4 us -> 0.01 us  [body(): lax.ppermute(tails, ('ctx', 'ch'), [(i, i + 1) for i in range(size - 1)])]
    convert_element_type x9 -> x5, other arithmetic: 20.2 us -> 2.46 us  [the longest x2 2.44 us: mode_table(): full.reshape(coarse.shape[0] * fine.shape[0], -1).astype(jnp.bfloat16)]
  transfers between devices with their start and end apart: 6 -> 4, of which waited for: 2 -> 2; matrix products, arithmetic and copies ran while one was open for 51% -> 16% of each run, Pallas kernels for 0% -> 0%
where the time goes in v1:
time: 153 us; the launch traced here: 150 us
  Pallas kernels  40.7 us (27%)
  blocking collectives  30.1 us (20%)
  waiting for transfers between devices  28.8 us (19%)
  other arithmetic  20.9 us (14%)
  starting transfers between devices  16.9 us (11%)
  local copies, waits for them, and re-layouts  12.5 us (8%)
    all_to_all x1, blocking collectives, body(): lax.all_to_all(conv.reshape(members, count, share), 'ch', split_axis=0, c...  30.1 us
    all_to_all x1, waiting for transfers between devices, body(): lax.all_to_all(gated, 'ch', split_axis=0, concat_axis=0)  22.4 us
    pallas_call x1, Pallas kernels, body(): pl.pallas_call(conv_kernel, grid=(lane_blocks,), in_specs=[signal_spec, p...  14.7 us
    pallas_call x1, Pallas kernels, body(): pl.pallas_call(summary_kernel, grid=(lane_blocks,), in_specs=[signal_spec...  11.3 us
    pallas_call x1, Pallas kernels, body(): pl.pallas_call(gate_kernel, grid=(width // tile,), in_specs=[rows_spec, r...  7.7 us
    pallas_call x1, Pallas kernels, body(): pl.pallas_call(mix_kernel, grid=(width // tile,), in_specs=[rows_spec, pr...  7.01 us
    all_to_all x1, waiting for transfers between devices, body(): gathered = lax.all_to_all(own, 'ctx', split_axis=0, concat_axis=0)  6.45 us
    all_to_all x1, starting transfers between devices, body(): lax.all_to_all(jnp.stack(incoming), 'ctx', split_axis=0, concat_axis=0)  5.59 us
  transfers between devices with their start and end apart: 4, of which 2 were waited for; matrix products, arithmetic and copies ran while one was open for 16% of the time, Pallas kernels for 0%

profile of v1, /device:TPU:12, one launch (start us, length us, event | category | flops | bytes accessed | tf_op | source)
XLA Modules:
  0.0 150.3 jit_solution(13234719052638102398)
XLA Ops:
  0.0 0.9 slice.76
  0.9 0.9 slice.77
  1.9 0.9 slice.78
  3.0 1.9 %collective-permute-start = (bf16[6,8192]{1,0:T(8,128)(2,1)S(1)}, bf16[6,8192]{1,0:T(8,128)(2,1)S(1)}, u32[]{:S(2)}, u32[]{:S(2)}) collective-permute-start(bf16[6,8192]{1,0:T(8,128)(2,1)S(1)} %pad_maximum_fusion.1), channel_id=1, source_target_pairs={{0,1},{1,2},{2,3},{3,4},{4,5},{5,6},{6,7},{7,8},{8,9},{9,10},{10,1... | collective-permute-start | bytes 294920 | tf_op jit(solution)/shard_map/ppermute | solution.py:147
  6.5 1.3 fusion.24
  11.2 0.7 pad_maximum_fusion.power_ref
  12.0 2.0 %fusion.8 = (f32[16,4096]{1,0:T(8,128)S(1)}, f32[16,4096]{1,0:T(8,128)S(1)}, f32[16,4096]{1,0:T(8,128)S(1)}, f32[16,4096]{1,0:T(8,128)S(1)}) fusion(f32[16]{0:T(128)S(1)} %rev.7, f32[4096]{0:T(1024)S(1)} %mul.605, f32[4096]{0:T(1024)S(1)} %neg.30, f32[16]{0:T(128)S(1)} %iota_convert_fusion), kind=kLoop, calls=%fused_computation.16 | loop fusion | flops 524288 | bytes 1081472 | tf_op jit(solution)/shard_map/mul | solution.py:18
  16.2 7.7 %shard_map.82 = bf16[4,128,2048]{2,1,0:T(8,128)(2,1)} custom-call(bf16[128,8192]{1,0:T(8,128)(2,1)} %k_ref.1, bf16[128,8192]{1,0:T(8,128)(2,1)} %v_ref.1, bf16[6,8192]{1,0:T(8,128)(2,1)} %copy-done.3, f32[3,3,8192]{2,1,0:T(4,128)} %taps_ref.3), custom_call_target="tpu_custom_call" | custom-call | flops 12582912 | bytes 6291456 | tf_op jit(solution)/shard_map/pallas_call | solution.py:155
  23.9 4.0 %all-to-all-start = ((bf16[4,128,2048]{2,1,0:T(8,128)(2,1)}), bf16[4,128,2048]{2,1,0:T(8,128)(2,1)S(1)}, u32[]{:S(2)}, u32[]{:S(2)}) async-start(bf16[4,128,2048]{2,1,0:T(8,128)(2,1)} %shard_map.82), calls=%async_computation | async-start | bytes 4194304 | tf_op jit(solution)/shard_map/all_to_all | solution.py:165
  27.8 2.6 %multiply_subtract_fusion = (f32[8,4096]{1,0:T(8,128)S(1)}, f32[8,4096]{1,0:T(8,128)S(1)}, f32[8,4096]{1,0:T(8,128)S(1)}, f32[8,4096]{1,0:T(8,128)}) fusion(f32[4096]{0:T(1024)} %constant.16.clone.1, f32[8]{0:T(128)} %get-tuple-element.46, f32[4096]{0:T(1024)} %constant.15.clone.1, f32[4096]{0:T(1024)S(1)} %mul.605, f32[4096]{0:T(1024)} %copy-done.4, ...), kind=kLoop, calls=%fused_computation.34 | loop fusion | flops 655360 | bytes 622656 | tf_op jit(solution)/shard_map/sub | solution.py:23
  30.5 1.2 subtract_convert_fusion
  31.7 22.4 %all-to-all-done = bf16[4,128,2048]{2,1,0:T(8,128)(2,1)S(1)} async-done(((bf16[4,128,2048]{2,1,0:T(8,128)(2,1)}), bf16[4,128,2048]{2,1,0:T(8,128)(2,1)S(1)}, u32[]{:S(2)}, u32[]{:S(2)}) %all-to-all-start) | async-done | bytes 2097184 | tf_op jit(solution)/shard_map/all_to_all | solution.py:165
  54.1 1.3 copy-done
  55.4 11.3 %shard_map.83 = (f32[128,2048]{1,0:T(8,128)}, f32[8,32,256]{2,1,0:T(8,128)}) custom-call(bf16[512,2048]{1,0:T(8,128)(2,1)} %bitcast.40, bf16[128,4096]{1,0:T(8,128)(2,1)} %bitcast.43, f32[32,2048]{1,0:T(8,128)} %pad_maximum_fusion.power_ref), custom_call_target="tpu_custom_call" | custom-call | tf_op jit(solution)/shard_map/pallas_call | solution.py:201
  66.7 5.4 %all-to-all-start.1 = ((f32[8,32,256]{2,1,0:T(8,128)}), f32[8,32,256]{2,1,0:T(8,128)S(1)}, u32[]{:S(2)}, u32[]{:S(2)}) async-start(f32[8,32,256]{2,1,0:T(8,128)} %get-tuple-element.8), calls=%async_computation.1 | async-start | bytes 524288 | tf_op jit(solution)/shard_map/all_to_all | solution.py:212
  72.9 6.5 %all-to-all-done.1 = f32[8,32,256]{2,1,0:T(8,128)S(1)} async-done(((f32[8,32,256]{2,1,0:T(8,128)}), f32[8,32,256]{2,1,0:T(8,128)S(1)}, u32[]{:S(2)}, u32[]{:S(2)}) %all-to-all-start.1) | async-done | bytes 262176 | tf_op jit(solution)/shard_map/all_to_all | solution.py:212
  83.8 5.6 %all-to-all-start.2 = ((f32[8,32,256]{2,1,0:T(8,128)}), f32[8,32,256]{2,1,0:T(8,128)S(1)}, u32[]{:S(2)}, u32[]{:S(2)}) async-start(f32[8,32,256]{2,1,0:T(8,128)} %fusion.14), calls=%async_computation.2 | async-start | bytes 524288 | tf_op jit(solution)/shard_map/all_to_all | solution.py:225
  89.4 1.2 subtract_convert_fusion.1
  91.0 1.3 dynamic_slice.23
  92.3 5.4 %fusion.3.taps_ref = f32[128,128]{1,0:T(8,128)} fusion(f32[128,16]{1,0:T(8,128)S(1)} %copy.24, f32[128,16]{1,0:T(8,128)S(1)} %copy.23, f32[128]{0:T(128)S(1)} %fusion.22, f32[128,16]{1,0:T(8,128)S(1)} %copy.22, f32[128,16]{1,0:T(8,128)S(1)} %copy.21), kind=kLoop, calls=%fused_computation.7 | loop fusion | flops 2080768 | bytes 98816 | tf_op jit(solution)/shard_map/reduce_sum | solution.py:189
  97.7 0.7 copy-done.1
  98.4 14.7 %shard_map.84 = bf16[512,2048]{1,0:T(8,128)(2,1)} custom-call(bf16[512,2048]{1,0:T(8,128)(2,1)} %bitcast.41, f32[128,128]{1,0:T(8,128)} %fusion.3.taps_ref, bf16[128,4096]{1,0:T(8,128)(2,1)} %bitcast.44, f32[128,2048]{1,0:T(8,128)} %get-tuple-element.7.earlier_ref, f32[8,32,256]{2,1,0:T(8,128)} %copy-done.1, f32[32,2048]{1,0:T(8,128)} %pad_maximum_fusion.power_ref, ...), custom_call_target="tpu_custom_call" | custom-call | tf_op jit(solution)/shard_map/pallas_call | solution.py:227
  113.1 30.1 %all_to_all.20.conv_ref = bf16[4,128,2048]{2,1,0:T(8,128)(2,1)} all-to-all(bf16[4,128,2048]{2,1,0:T(8,128)(2,1)} %bitcast.42), channel_id=1, replica_groups=mesh['ctx'=8,'ch'=4] {'ch'}, dimensions={0} | all-to-all | bytes 4194304 | tf_op jit(solution)/shard_map/all_to_all | solution.py:247
  143.2 7.0 %shard_map.85 = bf16[128,8192]{1,0:T(8,128)(2,1)} custom-call(bf16[128,8192]{1,0:T(8,128)(2,1)} %q_ref.1, bf16[6,8192]{1,0:T(8,128)(2,1)} %copy-done.3, f32[3,3,8192]{2,1,0:T(4,128)} %taps_ref.3, bf16[4,128,2048]{2,1,0:T(8,128)(2,1)} %all_to_all.20.conv_ref), custom_call_target="tpu_custom_call" | custom-call | tf_op jit(solution)/shard_map/pallas_call | solution.py:250
  (75 shorter events, 12.8 us)
Async XLA Ops:
  3.0 12.6 %collective-permute-start = (bf16[6,8192]{1,0:T(8,128)(2,1)S(1)}, bf16[6,8192]{1,0:T(8,128)(2,1)S(1)}, u32[]{:S(2)}, u32[]{:S(2)}) collective-permute-start(bf16[6,8192]{1,0:T(8,128)(2,1)S(1)} %pad_maximum_fusion.1), channel_id=1, source_target_pairs={{0,1},{1,2},{2,3},{3,4},{4,5},{5,6},{6,7},{7,8},{8,9},{9,10},{10,1... | collective-permute-start | bytes 294920 | tf_op jit(solution)/shard_map/ppermute | solution.py:147
  5.6 8.3 %copy-start.7 = (f32[128,16]{0,1:T(8,128)}, f32[128,16]{0,1:T(8,128)S(1)}, u32[]{:S(2)}) copy-start(f32[128,16]{0,1:T(8,128)S(1)} %dynamic-slice_bitcast_fusion.1) | copy-start | bytes 24580
  6.3 4.4 %copy-start.5 = (f32[128,16]{0,1:T(8,128)}, f32[128,16]{0,1:T(8,128)S(1)}, u32[]{:S(2)}) copy-start(f32[128,16]{0,1:T(8,128)S(1)} %get-tuple-element.44) | copy-start | bytes 24580
  6.3 7.6 %copy-start.9 = (f32[128,16]{0,1:T(8,128)}, f32[128,16]{0,1:T(8,128)S(1)}, u32[]{:S(2)}) copy-start(f32[128,16]{0,1:T(8,128)S(1)} %get-tuple-element.13) | copy-start | bytes 24580
  8.0 15.9 %copy-start.4 = (f32[4096]{0:T(1024)}, f32[4096]{0:T(1024)S(1)}, u32[]{:S(2)}) copy-start(f32[4096]{0:T(1024)S(1)} %neg.30) | copy-start | bytes 49156
  15.5 0.6 copy-start.3
  23.9 30.2 %all-to-all-start = ((bf16[4,128,2048]{2,1,0:T(8,128)(2,1)}), bf16[4,128,2048]{2,1,0:T(8,128)(2,1)S(1)}, u32[]{:S(2)}, u32[]{:S(2)}) async-start(bf16[4,128,2048]{2,1,0:T(8,128)(2,1)} %shard_map.82), calls=%async_computation | async-start | bytes 4194304 | tf_op jit(solution)/shard_map/all_to_all | solution.py:165
  54.1 1.3 copy-start
  66.7 22.7 %copy-start.2 = (f32[8,4096]{1,0:T(8,128)S(1)}, f32[8,4096]{1,0:T(8,128)}, u32[]{:S(2)}) copy-start(f32[8,4096]{1,0:T(8,128)} %get-tuple-element.39) | copy-start | bytes 393220
  66.7 12.6 %all-to-all-start.1 = ((f32[8,32,256]{2,1,0:T(8,128)}), f32[8,32,256]{2,1,0:T(8,128)S(1)}, u32[]{:S(2)}, u32[]{:S(2)}) async-start(f32[8,32,256]{2,1,0:T(8,128)} %get-tuple-element.8), calls=%async_computation.1 | async-start | bytes 524288 | tf_op jit(solution)/shard_map/all_to_all | solution.py:212
  79.3 11.3 %copy-start.6 = (f32[128,16]{0,1:T(8,128)S(1)}, f32[128,16]{0,1:T(8,128)}, u32[]{:S(2)}) copy-start(f32[128,16]{0,1:T(8,128)} %copy-done.5) | copy-start | bytes 24580
  79.3 11.3 %copy-start.10 = (f32[128,16]{0,1:T(8,128)S(1)}, f32[128,16]{0,1:T(8,128)}, u32[]{:S(2)}) copy-start(f32[128,16]{0,1:T(8,128)} %copy-done.9) | copy-start | bytes 24580
  79.3 11.4 %copy-start.8 = (f32[128,16]{0,1:T(8,128)S(1)}, f32[128,16]{0,1:T(8,128)}, u32[]{:S(2)}) copy-start(f32[128,16]{0,1:T(8,128)} %copy-done.7) | copy-start | bytes 24580
  79.4 11.5 %copy-start.11 = (f32[128,16]{0,1:T(8,128)S(1)}, f32[128,16]{0,1:T(8,128)}, u32[]{:S(2)}) copy-start(f32[128,16]{0,1:T(8,128)} %get-tuple-element.14) | copy-start | bytes 24580
  83.8 13.9 %all-to-all-start.2 = ((f32[8,32,256]{2,1,0:T(8,128)}), f32[8,32,256]{2,1,0:T(8,128)S(1)}, u32[]{:S(2)}, u32[]{:S(2)}) async-start(f32[8,32,256]{2,1,0:T(8,128)} %fusion.14), calls=%async_computation.2 | async-start | bytes 524288 | tf_op jit(solution)/shard_map/all_to_all | solution.py:225
  97.7 0.7 copy-start.1
